TPU v7x, 32 devices: a whole 2x2x4 slice. The times are simulated.
32 devices in a mesh: tm: 8 (over z, y), head: 4 (over x, core).
Axes of the slice: x: 2, y: 2, z: 4, core: 2. Of those that a mesh axis runs over, the one named last changes fastest.
Arguments:
- queries: bfloat16 [6144, 1536], P('tm', 'head'), may hold values from -6 to 6
- key_rows: bfloat16 [6144, 1536], P('tm', 'head'), may hold values from -6 to 6
- value_rows: bfloat16 [6144, 1536], P('tm', 'head'), may hold values from -6 to 6
- grad_out: bfloat16 [6144, 3072], P('tm', 'head'), may hold values from -192 to 192
- w_out: bfloat16 [1536, 3072], P('head', 'tm'), may hold values from -0.109375 to 0.109375
Outputs:
- grad_queries: bfloat16 [6144, 1536], P('tm', 'head')
- grad_keys: bfloat16 [6144, 1536], P('tm', 'head')
- grad_values: bfloat16 [6144, 1536], P('tm', 'head')
All inputs are finite; a program needn't handle non-finite values.
Results may differ from a plain program's by a relative error of at most 0.0081.
Values may be sent and summed in bfloat16 or wider, within the bound.
No kernel may reach another device: no remote copies, remote signals or barrier semaphores. Data moves between devices by JAX's collectives and lax.ppermute only.
A program may use at most 128 MiB of HBM per device.

v0:
```python
import math
import jax
import jax.numpy as jnp
from jax import lax
from jax.sharding import PartitionSpec as P

HD = 128
TILE_T = 6
TILE_H = 8
TILE_W = 8
VT = 8


def passed_along(block, axis, distance):
    devices = range(lax.axis_size(axis))
    route = [(i - distance, i) for i in devices if i - distance in devices]
    return lax.ppermute(block, axis, route)


def tile_range(index, count):
    return (max(index - 1, 0), min(index + 1, count - 1))


def local(queries, key_rows, value_rows, grad_out, w_out):
    token_count, local_width = queries.shape
    head_count = local_width // HD
    tile_size = TILE_T * TILE_H * TILE_W
    tile_count = token_count // tile_size
    inverse_root = 1.0 / math.sqrt(HD)
    video_place = lax.axis_index("tm") % VT
    flags = (video_place > 0, video_place >= 0, video_place < VT - 1)
    full_grad = lax.all_gather(grad_out, "head", axis=1, tiled=True)
    attn_sum = jnp.einsum(
        "td,hd->th",
        full_grad,
        lax.all_gather(w_out, "tm", axis=1, tiled=True),
        preferred_element_type=jnp.float32,
    )
    attn_grad = attn_sum.astype(jnp.bfloat16)
    before_keys, before_values = passed_along((key_rows, value_rows), "tm", 1)
    after_keys, after_values = passed_along((key_rows, value_rows), "tm", -1)
    slab_keys = (before_keys, key_rows, after_keys)
    slab_values = (before_values, value_rows, after_values)
    zero_tile = jnp.zeros((tile_size, local_width), jnp.float32)
    key_sums = [[zero_tile] * tile_count for other in range(3)]
    value_sums = [[zero_tile] * tile_count for other in range(3)]
    query_grads = []
    for tile_index in range(tile_count):
        lower, upper = tile_range(tile_index, tile_count)
        width_rows = (upper - lower + 1) * tile_size
        key_block = jnp.concatenate([part for part in slab_keys], 0)
        key_block = key_block.reshape(3 * width_rows, head_count, HD)
        value_block = jnp.concatenate([part for part in slab_values], 0)
        value_block = value_block.reshape(3 * width_rows, head_count, HD)
        key_mask = jnp.concatenate([jnp.broadcast_to(flag, (width_rows,)) for flag in flags], 0)
        query_tile = queries[tile_index * tile_size : (tile_index + 1) * tile_size].reshape(
            tile_size, head_count, HD
        )
        grad_tile = attn_grad[tile_index * tile_size : (tile_index + 1) * tile_size].reshape(
            tile_size, head_count, HD
        )
        scores = (
            jnp.einsum("qhd,khd->hqk", query_tile, key_block, preferred_element_type=jnp.float32)
            * inverse_root
        )
        scores = jnp.where(key_mask[None, None, :], scores, -jnp.inf)
        row_peak = jnp.max(scores, axis=2, keepdims=True)
        weights = jnp.exp(scores - row_peak)
        row_total = jnp.sum(weights, axis=2, keepdims=True)
        softmax_rows = weights / row_total
        softmax_grad = jnp.einsum(
            "qhd,khd->hqk", grad_tile, value_block, preferred_element_type=jnp.float32
        )
        row_inner = jnp.sum(softmax_rows * softmax_grad, axis=2, keepdims=True)
        score_grad = (softmax_rows * (softmax_grad - row_inner)).astype(jnp.bfloat16)
        softmax_low = softmax_rows.astype(jnp.bfloat16)
        grad_query = (
            jnp.einsum("hqk,khd->qhd", score_grad, key_block, preferred_element_type=jnp.float32)
            * inverse_root
        )
        query_grads.append(grad_query.reshape(tile_size, local_width).astype(jnp.bfloat16))
        kept = (0, 1, 2)
        key_part = (
            jnp.einsum("hqk,qhd->khd", score_grad, query_tile, preferred_element_type=jnp.float32)
            * inverse_root
        )
        key_part = key_part.reshape(len(kept) * width_rows, local_width)
        value_part = jnp.einsum(
            "hqk,qhd->khd", softmax_low, grad_tile, preferred_element_type=jnp.float32
        )
        value_part = value_part.reshape(len(kept) * width_rows, local_width)
        for position, slab_index in enumerate(kept):
            for neighbour in range(lower, upper + 1):
                offset = position * width_rows + (neighbour - lower) * tile_size
                key_sums[slab_index][neighbour] = (
                    key_sums[slab_index][neighbour] + key_part[offset : offset + tile_size]
                )
                value_sums[slab_index][neighbour] = (
                    value_sums[slab_index][neighbour] + value_part[offset : offset + tile_size]
                )
    own_keys = jnp.concatenate(key_sums[1], 0)
    own_values = jnp.concatenate(value_sums[1], 0)
    later_keys, later_values = (
        passed_along(jnp.concatenate(key_sums[0], 0).astype(jnp.bfloat16), "tm", -1).astype(
            jnp.float32
        ),
        passed_along(jnp.concatenate(value_sums[0], 0).astype(jnp.bfloat16), "tm", -1).astype(
            jnp.float32
        ),
    )
    earlier_keys, earlier_values = (
        passed_along(jnp.concatenate(key_sums[2], 0).astype(jnp.bfloat16), "tm", 1).astype(
            jnp.float32
        ),
        passed_along(jnp.concatenate(value_sums[2], 0).astype(jnp.bfloat16), "tm", 1).astype(
            jnp.float32
        ),
    )
    grad_keys = own_keys + later_keys + earlier_keys
    grad_values = own_values + later_values + earlier_values
    grad_queries = jnp.concatenate(query_grads, 0)
    return (grad_queries, grad_keys.astype(jnp.bfloat16), grad_values.astype(jnp.bfloat16))


def solution(mesh):
    placed = (P("tm", "head"), P("tm", "head"), P("tm", "head"), P("tm", "head"), P("head", "tm"))
    return jax.shard_map(
        local,
        mesh=mesh,
        in_specs=placed,
        out_specs=(P("tm", "head"), P("tm", "head"), P("tm", "head")),
        check_vma=False,
    )
```

profile of v0, /device:TPU:0, one launch (start us, length us, event | category | flops | bytes accessed | tf_op | source)
XLA Modules:
  0.0 249.1 jit_solution(441162464719006397)
XLA Ops:
  7.2 0.7 all-gather.5.cloned.1.call-update
  8.0 0.7 all-gather.3.cloned.1.call-update
  8.7 1.3 copy.44
  10.0 1.3 collective-permute-start.3
  11.3 6.4 %collective-permute-start.2 = (bf16[768,384]{0,1:T(8,128)(2,1)S(1)}, bf16[768,384]{0,1:T(8,128)(2,1)}, u32[]{:S(2)}, u32[]{:S(2)}) collective-permute-start(bf16[768,384]{0,1:T(8,128)(2,1)S(1)} %copy.44), channel_id=1, source_target_pairs={{0,4},{4,8},{8,12},{12,16},{16,20},{20,24},{24,28},{1,5},{5,9},{9,... | collective-permute-start | bytes 1769480 | tf_op jit(solution)/shard_map/ppermute | solution.py:17
  17.6 1.3 copy.38
  18.9 1.3 collective-permute-start.1
  20.2 5.4 %collective-permute-start = (bf16[768,384]{0,1:T(8,128)(2,1)S(1)}, bf16[768,384]{0,1:T(8,128)(2,1)}, u32[]{:S(2)}, u32[]{:S(2)}) collective-permute-start(bf16[768,384]{0,1:T(8,128)(2,1)S(1)} %copy.38), channel_id=1, source_target_pairs={{0,4},{4,8},{8,12},{12,16},{16,20},{20,24},{24,28},{1,5},{5,9},{9,... | collective-permute-start | bytes 1769480 | tf_op jit(solution)/shard_map/ppermute | solution.py:17
  25.8 0.2 copy.94
  26.0 0.2 copy.95
  26.3 5.9 %collective-permute-done.3 = bf16[768,384]{0,1:T(8,128)(2,1)S(1)} collective-permute-done((bf16[768,384]{0,1:T(8,128)(2,1)S(1)}, bf16[768,384]{0,1:T(8,128)(2,1)S(1)}, u32[]{:S(2)}, u32[]{:S(2)}) %collective-permute-start.3) | collective-permute-done | bytes 589856 | tf_op jit(solution)/shard_map/ppermute | solution.py:17
  32.2 24.7 %collective-permute-done.2 = bf16[768,384]{0,1:T(8,128)(2,1)} collective-permute-done((bf16[768,384]{0,1:T(8,128)(2,1)S(1)}, bf16[768,384]{0,1:T(8,128)(2,1)}, u32[]{:S(2)}, u32[]{:S(2)}) %collective-permute-start.2) | collective-permute-done | bytes 589856 | tf_op jit(solution)/shard_map/ppermute | solution.py:17
  56.9 2.5 pad_maximum_fusion.1
  59.4 0.8 copy-done.4
  60.2 11.8 %collective-permute-done = bf16[768,384]{0,1:T(8,128)(2,1)} collective-permute-done((bf16[768,384]{0,1:T(8,128)(2,1)S(1)}, bf16[768,384]{0,1:T(8,128)(2,1)}, u32[]{:S(2)}, u32[]{:S(2)}) %collective-permute-start) | collective-permute-done | bytes 589856 | tf_op jit(solution)/shard_map/ppermute | solution.py:17
  72.0 1.4 pad_maximum_fusion
  73.4 7.7 %fusion.52 = (f32[3,384]{1,0:T(4,128)S(1)}, f32[3,384,2304]{1,2,0:T(8,128)}) fusion(pred[2304]{0:T(1024)(128)(4,1)S(1)} %pad_add_fusion, bf16[2304,3,128]{0,2,1:T(8,128)(2,1)S(1)} %bitcast.78, bf16[384,3,128]{0,2,1:T(8,128)(2,1)S(1)} %bitcast.95), kind=kOutput, calls=%fused_computation.81 | convolution fusion | flops 690096384 | bytes 12688128 | tf_op jit(solution)/shard_map/sub | solution.py:68
  81.0 7.8 %fusion.53 = (f32[3,384]{1,0:T(4,128)S(1)}, f32[3,384,2304]{1,2,0:T(8,128)}) fusion(pred[2304]{0:T(1024)(128)(4,1)S(1)} %pad_add_fusion, bf16[2304,3,128]{0,2,1:T(8,128)(2,1)S(1)} %bitcast.79, bf16[384,3,128]{0,2,1:T(8,128)(2,1)S(1)} %bitcast.92), kind=kOutput, calls=%fused_computation.82 | convolution fusion | flops 690096384 | bytes 12688128 | tf_op jit(solution)/shard_map/sub | solution.py:68
  88.9 3.6 %all-gather.5.cloned.1.call-done = bf16[384,3072]{1,0:T(8,128)(2,1)} async-done(((bf16[384,384]{1,0:T(8,128)(2,1)}), bf16[384,3072]{1,0:T(8,128)(2,1)}) %all-gather.5.cloned.1.call-update) | async-done | bytes 2359312 | tf_op jit(solution)/shard_map/all_gather | solution.py:36
  92.5 39.1 %all-gather.3.cloned.1.call-done = bf16[768,3072]{1,0:T(8,128)(2,1)} async-done(((bf16[768,768]{1,0:T(8,128)(2,1)}), bf16[768,3072]{1,0:T(8,128)(2,1)}) %all-gather.3.cloned.1.call-update) | async-done | bytes 4718608 | tf_op jit(solution)/shard_map/all_gather | solution.py:32
  131.6 5.1 %convolution_convert_fusion = bf16[768,384]{0,1:T(8,128)(2,1)S(1)} fusion(bf16[768,3072]{1,0:T(8,128)(2,1)} %all-gather.3.cloned.1.call-done, bf16[384,3072]{1,0:T(8,128)(2,1)} %all-gather.5.cloned.1.call-done), kind=kOutput, calls=%fused_computation.36 | convolution fusion | flops 1812234240 | bytes 7667712 | tf_op jit(solution)/shard_map/td,hd->th/dot_general | solution.py:33
  136.8 5.8 %fusion.25 = f32[2304,3,128]{0,2,1:T(8,128)S(1)} fusion(bf16[384,3,128]{0,2,1:T(8,128)(2,1)S(1)} %bitcast.108, f32[3,384,2304]{1,2,0:T(8,128)} %get-tuple-element.20, f32[3,384]{1,0:T(4,128)S(1)} %get-tuple-element.19), kind=kOutput, calls=%fused_computation.33 | convolution fusion | flops 684785664 | bytes 14455296 | tf_op jit(solution)/shard_map/hqk,qhd->khd/dot_general | solution.py:88
  142.6 0.6 slice-done.4
  143.2 0.6 slice-done.5
  143.9 0.5 copy-done.3
  144.3 5.0 %multiply_reduce_fusion = (f32[3,384]{1,0:T(4,128)S(1)}, f32[3,384,2304]{1,2,0:T(8,128)}) fusion(f32[3,384,2304]{1,2,0:T(8,128)S(1)} %bitcast.85, f32[3,384]{1,0:T(4,128)S(1)} %get-tuple-element.19, bf16[384,3,128]{0,2,1:T(8,128)(2,1)S(1)} %bitcast.109, bf16[2304,3,128]{0,2,1:T(8,128)(2,1)S(1)} %bitcast.90), kind=kOutput, calls=%fused_computation.11 | convolution fusion | flops 687438720 | bytes 23307264 | tf_op jit(solution)/shard_map/qhd,khd->hqk/dot_general | solution.py:71
  149.4 8.3 %multiply_convert_fusion = bf16[3,384,2304]{1,2,0:T(8,128)(2,1)S(1)} fusion(f32[3,384,2304]{1,2,0:T(8,128)} %get-tuple-element.22, f32[3,384]{1,0:T(4,128)S(1)} %get-tuple-element.21, f32[3,384,2304]{1,2,0:T(8,128)} %get-tuple-element.20, f32[3,384]{1,0:T(4,128)S(1)} %get-tuple-element.19), kind=kLoop, calls=%fused_computation.10 | loop fusion | flops 10616832 | bytes 26551296 | tf_op jit(solution)/shard_map/convert_element_type | solution.py:75
  157.7 1.9 fusion.29
  159.5 3.4 %fusion.21 = f32[2304,3,128]{0,2,1:T(8,128)} fusion(bf16[3,384,2304]{1,2,0:T(8,128)(2,1)S(1)} %multiply_convert_fusion, bf16[384,3,128]{0,2,1:T(8,128)(2,1)S(1)} %bitcast.96), kind=kOutput, calls=%fused_computation.31 | convolution fusion | flops 680361984 | bytes 9142272 | tf_op jit(solution)/shard_map/hqk,qhd->khd/dot_general | solution.py:84
  162.9 1.6 fusion.22
  164.5 5.0 %multiply_reduce_fusion.1 = (f32[3,384]{1,0:T(4,128)S(1)}, f32[3,384,2304]{1,2,0:T(8,128)}) fusion(f32[3,384,2304]{1,2,0:T(8,128)S(1)} %bitcast.83, f32[3,384]{1,0:T(4,128)S(1)} %get-tuple-element.23, bf16[384,3,128]{0,2,1:T(8,128)(2,1)S(1)} %bitcast.107, bf16[2304,3,128]{0,2,1:T(8,128)(2,1)S(1)} %bitcast.91), kind=kOutput, calls=%fused_computation.14 | convolution fusion | flops 687438720 | bytes 23307264 | tf_op jit(solution)/shard_map/qhd,khd->hqk/dot_general | solution.py:71
  169.5 1.2 fusion.41
  170.7 1.9 copy.74
  172.6 1.8 copy.77
  174.4 1.8 copy.76
  176.3 0.9 copy.75
  177.2 2.0 pad_maximum_fusion.5
  179.2 1.3 collective-permute-start.6
  180.5 1.9 pad_maximum_fusion.6
  182.4 5.4 %collective-permute-start.7 = (bf16[768,384]{1,0:T(8,128)(2,1)}, bf16[768,384]{1,0:T(8,128)(2,1)}, u32[]{:S(2)}, u32[]{:S(2)}) collective-permute-start(bf16[768,384]{1,0:T(8,128)(2,1)} %pad_maximum_fusion.6), channel_id=1, source_target_pairs={{0,4},{4,8},{8,12},{12,16},{16,20},{20,24},{24,28},{1,5},{5,9},{9,... | collective-permute-start | bytes 1769480 | tf_op jit(solution)/shard_map/ppermute | solution.py:17
  187.7 7.9 %multiply_convert_fusion.1 = bf16[3,384,2304]{1,2,0:T(8,128)(2,1)S(1)} fusion(f32[3,384,2304]{1,2,0:T(8,128)} %get-tuple-element.26, f32[3,384]{1,0:T(4,128)S(1)} %get-tuple-element.25, f32[3,384,2304]{1,2,0:T(8,128)} %get-tuple-element.24, f32[3,384]{1,0:T(4,128)S(1)} %get-tuple-element.23), kind=kLoop, calls=%fused_computation.13 | loop fusion | flops 10616832 | bytes 26551296 | tf_op jit(solution)/shard_map/convert_element_type | solution.py:75
  195.7 1.6 fusion.20
  197.3 1.1 copy-done
  198.4 1.2 copy-done.1
  199.6 1.4 fusion.45
  201.0 1.9 copy.66
  202.8 1.9 copy.69
  204.7 1.9 copy.68
  206.5 1.8 copy.67
  208.4 1.9 pad_maximum_fusion.3
  210.3 1.3 collective-permute-start.4
  211.6 1.9 pad_maximum_fusion.4
  213.5 5.4 %collective-permute-start.5 = (bf16[768,384]{1,0:T(8,128)(2,1)}, bf16[768,384]{1,0:T(8,128)(2,1)}, u32[]{:S(2)}, u32[]{:S(2)}) collective-permute-start(bf16[768,384]{1,0:T(8,128)(2,1)} %pad_maximum_fusion.4), channel_id=1, source_target_pairs={{0,4},{4,8},{8,12},{12,16},{16,20},{20,24},{24,28},{1,5},{5,9},{9,... | collective-permute-start | bytes 1769480 | tf_op jit(solution)/shard_map/ppermute | solution.py:17
  218.9 4.3 %fusion.28 = bf16[3,128,384]{2,1,0:T(8,128)(2,1)} fusion(bf16[2304,3,128]{0,2,1:T(8,128)(2,1)S(1)} %bitcast.81, bf16[3,384,2304]{1,2,0:T(8,128)(2,1)} %copy-done), kind=kOutput, calls=%fused_computation.39 | convolution fusion | flops 679772160 | bytes 7372800 | tf_op jit(solution)/shard_map/hqk,khd->qhd/dot_general | solution.py:78
  223.2 1.9 copy.61
  225.1 0.2 copy.73
  225.4 0.2 copy.72
  225.6 1.2 copy.60
  226.8 0.2 copy.65
  227.0 0.2 copy.64
  227.3 1.8 pad_maximum_fusion.2
  229.1 2.2 fusion.33
  231.4 8.7 %collective-permute-done.5 = bf16[768,384]{1,0:T(8,128)(2,1)} collective-permute-done((bf16[768,384]{1,0:T(8,128)(2,1)}, bf16[768,384]{1,0:T(8,128)(2,1)}, u32[]{:S(2)}, u32[]{:S(2)}) %collective-permute-start.5) | collective-permute-done | bytes 589856 | tf_op jit(solution)/shard_map/ppermute | solution.py:17
  240.0 2.2 fusion.31
  (32 shorter events, 0.3 us)
Async XLA Ops:
  7.2 18.5 %copy-start.5 = (bf16[768,384]{1,0:T(8,128)(2,1)S(1)}, bf16[768,384]{1,0:T(8,128)(2,1)}, u32[]{:S(2)}) copy-start(bf16[768,384]{1,0:T(8,128)(2,1)} %param.5) | copy-start | bytes 1769476
  7.2 85.3 %all-gather.5.cloned.1.call-start = ((), (), s32[]{:S(2)}) async-start(), calls=%async_computation.1 | async-start | bytes 2654208 | tf_op jit(solution)/shard_map/all_gather | solution.py:36
  7.9 123.7 %all-gather.3.cloned.1.call-start = ((), (), s32[]{:S(2)}) async-start(), calls=%async_computation | async-start | bytes 5898240 | tf_op jit(solution)/shard_map/all_gather | solution.py:32
  10.0 22.2 %collective-permute-start.3 = (bf16[768,384]{0,1:T(8,128)(2,1)S(1)}, bf16[768,384]{0,1:T(8,128)(2,1)S(1)}, u32[]{:S(2)}, u32[]{:S(2)}) collective-permute-start(bf16[768,384]{0,1:T(8,128)(2,1)S(1)} %copy.44), channel_id=1, source_target_pairs={{4,0},{8,4},{12,8},{16,12},{20,16},{24,20},{28,24},{5,1},{9,5},{13... | collective-permute-start | bytes 1769480 | tf_op jit(solution)/shard_map/ppermute | solution.py:17
  11.3 45.6 %collective-permute-start.2 = (bf16[768,384]{0,1:T(8,128)(2,1)S(1)}, bf16[768,384]{0,1:T(8,128)(2,1)}, u32[]{:S(2)}, u32[]{:S(2)}) collective-permute-start(bf16[768,384]{0,1:T(8,128)(2,1)S(1)} %copy.44), channel_id=1, source_target_pairs={{0,4},{4,8},{8,12},{12,16},{16,20},{20,24},{24,28},{1,5},{5,9},{9,... | collective-permute-start | bytes 1769480 | tf_op jit(solution)/shard_map/ppermute | solution.py:17
  18.9 40.4 %collective-permute-start.1 = (bf16[768,384]{0,1:T(8,128)(2,1)S(1)}, bf16[768,384]{0,1:T(8,128)(2,1)S(1)}, u32[]{:S(2)}, u32[]{:S(2)}) collective-permute-start(bf16[768,384]{0,1:T(8,128)(2,1)S(1)} %copy.38), channel_id=1, source_target_pairs={{4,0},{8,4},{12,8},{16,12},{20,16},{24,20},{28,24},{5,1},{9,5},{13... | collective-permute-start | bytes 1769480 | tf_op jit(solution)/shard_map/ppermute | solution.py:17
  20.2 51.8 %collective-permute-start = (bf16[768,384]{0,1:T(8,128)(2,1)S(1)}, bf16[768,384]{0,1:T(8,128)(2,1)}, u32[]{:S(2)}, u32[]{:S(2)}) collective-permute-start(bf16[768,384]{0,1:T(8,128)(2,1)S(1)} %copy.38), channel_id=1, source_target_pairs={{0,4},{4,8},{8,12},{12,16},{16,20},{20,24},{24,28},{1,5},{5,9},{9,... | collective-permute-start | bytes 1769480 | tf_op jit(solution)/shard_map/ppermute | solution.py:17
  59.4 0.8 copy-start.4
  136.7 5.9 %slice-start.3 = ((s8[10616832]{0:T(1024)(128)(4,1)}), s8[4194304]{0:T(1024)(128)(4,1)S(1)}, s32[]{:S(2)}) async-start(s8[10616832]{0:T(1024)(128)(4,1)} %bitcast.84), calls=%async_computation.5 | async-start | bytes 8388608
  136.8 6.4 %slice-start.4 = ((s8[10616832]{0:T(1024)(128)(4,1)}), s8[4194304]{0:T(1024)(128)(4,1)S(1)}, s32[]{:S(2)}) async-start(s8[10616832]{0:T(1024)(128)(4,1)} %bitcast.84), calls=%async_computation.6 | async-start | bytes 8388608
  136.8 7.1 %slice-start.5 = ((s8[10616832]{0:T(1024)(128)(4,1)}), s8[2228224]{0:T(1024)(128)(4,1)S(1)}, s32[]{:S(2)}) async-start(s8[10616832]{0:T(1024)(128)(4,1)} %bitcast.84), calls=%async_computation.7 | async-start | bytes 4456448
  136.8 7.5 %copy-start.3 = (bf16[2304,384]{0,1:T(8,128)(2,1)S(1)}, bf16[2304,384]{0,1:T(8,128)(2,1)}, u32[]{:S(2)}) copy-start(bf16[2304,384]{0,1:T(8,128)(2,1)} %pad_maximum_fusion.1) | copy-start | bytes 5308420
  149.4 13.5 %slice-start = ((s8[10616832]{0:T(1024)(128)(4,1)}), s8[4194304]{0:T(1024)(128)(4,1)S(1)}, s32[]{:S(2)}) async-start(s8[10616832]{0:T(1024)(128)(4,1)} %bitcast.82), calls=%async_computation.2 | async-start | bytes 8388608
  149.4 13.5 %slice-start.1 = ((s8[10616832]{0:T(1024)(128)(4,1)}), s8[4194304]{0:T(1024)(128)(4,1)S(1)}, s32[]{:S(2)}) async-start(s8[10616832]{0:T(1024)(128)(4,1)} %bitcast.82), calls=%async_computation.3 | async-start | bytes 8388608
  157.7 5.2 %slice-start.2 = ((s8[10616832]{0:T(1024)(128)(4,1)}), s8[2228224]{0:T(1024)(128)(4,1)S(1)}, s32[]{:S(2)}) async-start(s8[10616832]{0:T(1024)(128)(4,1)} %bitcast.82), calls=%async_computation.4 | async-start | bytes 4456448
  179.2 49.9 %collective-permute-start.6 = (bf16[768,384]{1,0:T(8,128)(2,1)}, bf16[768,384]{1,0:T(8,128)(2,1)}, u32[]{:S(2)}, u32[]{:S(2)}) collective-permute-start(bf16[768,384]{1,0:T(8,128)(2,1)} %pad_maximum_fusion.5), channel_id=1, source_target_pairs={{4,0},{8,4},{12,8},{16,12},{20,16},{24,20},{28,24},{5,1},{9,5},{13... | collective-permute-start | bytes 1769480 | tf_op jit(solution)/shard_map/ppermute | solution.py:17
  182.4 46.7 %collective-permute-start.7 = (bf16[768,384]{1,0:T(8,128)(2,1)}, bf16[768,384]{1,0:T(8,128)(2,1)}, u32[]{:S(2)}, u32[]{:S(2)}) collective-permute-start(bf16[768,384]{1,0:T(8,128)(2,1)} %pad_maximum_fusion.6), channel_id=1, source_target_pairs={{0,4},{4,8},{8,12},{12,16},{16,20},{20,24},{24,28},{1,5},{5,9},{9,... | collective-permute-start | bytes 1769480 | tf_op jit(solution)/shard_map/ppermute | solution.py:17
  195.7 2.7 %copy-start = (bf16[3,384,2304]{1,2,0:T(8,128)(2,1)}, bf16[3,384,2304]{1,2,0:T(8,128)(2,1)S(1)}, u32[]{:S(2)}) copy-start(bf16[3,384,2304]{1,2,0:T(8,128)(2,1)S(1)} %multiply_convert_fusion.1) | copy-start | bytes 15925252
  195.7 3.9 %copy-start.1 = (f32[2304,3,128]{0,2,1:T(8,128)S(1)}, f32[2304,3,128]{0,2,1:T(8,128)}, u32[]{:S(2)}) copy-start(f32[2304,3,128]{0,2,1:T(8,128)} %fusion.21) | copy-start | bytes 10616836
  210.3 21.0 %collective-permute-start.4 = (bf16[768,384]{1,0:T(8,128)(2,1)}, bf16[768,384]{1,0:T(8,128)(2,1)}, u32[]{:S(2)}, u32[]{:S(2)}) collective-permute-start(bf16[768,384]{1,0:T(8,128)(2,1)} %pad_maximum_fusion.3), channel_id=1, source_target_pairs={{4,0},{8,4},{12,8},{16,12},{20,16},{24,20},{28,24},{5,1},{9,5},{13... | collective-permute-start | bytes 1769480 | tf_op jit(solution)/shard_map/ppermute | solution.py:17
  213.5 26.5 %collective-permute-start.5 = (bf16[768,384]{1,0:T(8,128)(2,1)}, bf16[768,384]{1,0:T(8,128)(2,1)}, u32[]{:S(2)}, u32[]{:S(2)}) collective-permute-start(bf16[768,384]{1,0:T(8,128)(2,1)} %pad_maximum_fusion.4), channel_id=1, source_target_pairs={{0,4},{4,8},{8,12},{12,16},{16,20},{20,24},{24,28},{1,5},{5,9},{9,... | collective-permute-start | bytes 1769480 | tf_op jit(solution)/shard_map/ppermute | solution.py:17
  223.2 3.6 %copy-start.2 = (f32[384,3,128]{0,2,1:T(8,128)S(1)}, f32[384,3,128]{0,2,1:T(8,128)}, u32[]{:S(2)}) copy-start(f32[384,3,128]{0,2,1:T(8,128)} %get-tuple-element.13) | copy-start | bytes 1769476
Sparse Core Ops, SparseCore 0:
  10.0 82.4 all-gather.4
  94.1 37.4 all-gather.2
where the time goes:
time: 250 us; the launch traced here: 249 us
  waiting for transfers between devices  95.2 us (38%)
  matrix products  49.2 us (20%)
  other arithmetic  36.7 us (15%)
  starting transfers between devices  27.8 us (11%)
  local copies, waits for them, and re-layouts  25.9 us (10%)
  between operations  14.3 us (6%)
    ppermute x8, waiting for transfers between devices, passed_along(): return lax.ppermute(block, axis, route)  51.1 us
    all_gather x1, waiting for transfers between devices, local(): full_grad = lax.all_gather(grad_out, 'head', axis=1, tiled=True)  39.1 us
    ppermute x8, starting transfers between devices, passed_along(): return lax.ppermute(block, axis, route)  27.7 us
    convert_element_type x2, other arithmetic, local(): (softmax_rows * (softmax_grad - row_inner)).astype(jnp.bfloat16)  16.2 us
    sub x2, matrix products, local(): weights = jnp.exp(scores - row_peak)  15.5 us
    dot_general x2, matrix products, local(): jnp.einsum('qhd,khd->hqk', grad_tile, value_block, preferred_element_type...  9.98 us
    add x6, local copies, waits for them, and re-layouts, local(): key_sums[slab_index][neighbour] + key_part[offset:offset + tile_size]  7.88 us
    unnamed x28, local copies, waits for them, and re-layouts  7.88 us
  transfers between devices with their start and end apart: 10, of which 6 were waited for; matrix products, arithmetic and copies ran while one was open for 24% of the time, Pallas kernels for 0%

commit v1 on v0

--- a/solution.py
+++ b/solution.py
@@ -9,6 +9,19 @@
 TILE_H = 8
 TILE_W = 8
 VT = 8
+
+
+def ring_gather(value, axis, dim):
+    ways = lax.axis_size(axis)
+    up = [(d, (d + 1) % ways) for d in range(ways)]
+    down = [(d, (d - 1) % ways) for d in range(ways)]
+    earlier, later = ([value], [value])
+    for _ in range(ways // 2):
+        earlier.append(lax.ppermute(earlier[-1], axis, up))
+    for _ in range((ways - 1) // 2):
+        later.append(lax.ppermute(later[-1], axis, down))
+    line = jnp.concatenate([*earlier[::-1], *later[1:]], axis=dim)
+    return jnp.roll(line, (lax.axis_index(axis) - ways // 2) * value.shape[dim], axis=dim)
 
 
 def passed_along(block, axis, distance):
@@ -29,7 +42,7 @@
     inverse_root = 1.0 / math.sqrt(HD)
     video_place = lax.axis_index("tm") % VT
     flags = (video_place > 0, video_place >= 0, video_place < VT - 1)
-    full_grad = lax.all_gather(grad_out, "head", axis=1, tiled=True)
+    full_grad = ring_gather(grad_out, "head", 1)
     attn_sum = jnp.einsum(
         "td,hd->th",
         full_grad,

time: 250 us -> 219 us (0.88)
  waiting for transfers between devices: 95.2 us -> 42 us
  local copies, waits for them, and re-layouts: 25.9 us -> 42.5 us
  starting transfers between devices: 27.8 us -> 30.9 us
    all_gather x1 -> x0, waiting for transfers between devices: 39.1 us -> none  [local(): full_grad = lax.all_gather(grad_out, 'head', axis=1, tiled=True)]
    unnamed x28 -> x43, local copies, waits for them, and re-layouts: 7.88 us -> 22.7 us
    ppermute x8, waiting for transfers between devices: 51.1 us -> 41.3 us  [passed_along(): return lax.ppermute(block, axis, route)]
    all_gather x1, waiting for transfers between devices: 3.64 us -> 0.01 us  [local(): lax.all_gather(w_out, 'tm', axis=1, tiled=True)]
    ppermute x0 -> x3, starting transfers between devices: none -> 2.61 us  [the longest x1 1.72 us: ring_gather(): later.append(lax.ppermute(later[-1], axis, down))]
  transfers between devices with their start and end apart: 10 -> 12, of which waited for: 6 -> 4; matrix products, arithmetic and copies ran while one was open for 24% -> 37% of each run, Pallas kernels for 0% -> 0%
where the time goes in v1:
time: 219 us; the launch traced here: 218 us
  matrix products  51.6 us (24%)
  local copies, waits for them, and re-layouts  42.5 us (19%)
  waiting for transfers between devices  42 us (19%)
  other arithmetic  36.9 us (17%)
  starting transfers between devices  30.9 us (14%)
  between operations  14.3 us (7%)
    ppermute x8, waiting for transfers between devices, passed_along(): return lax.ppermute(block, axis, route)  41.3 us
    ppermute x8, starting transfers between devices, passed_along(): return lax.ppermute(block, axis, route)  28.2 us
    unnamed x43, local copies, waits for them, and re-layouts  22.7 us
    sub x2, matrix products, local(): weights = jnp.exp(scores - row_peak)  17.4 us
    convert_element_type x2, other arithmetic, local(): (softmax_rows * (softmax_grad - row_inner)).astype(jnp.bfloat16)  16.2 us
    dot_general x2, matrix products, local(): jnp.einsum('qhd,khd->hqk', grad_tile, value_block, preferred_element_type...  9.94 us
    add x6, local copies, waits for them, and re-layouts, local(): key_sums[slab_index][neighbour] + key_part[offset:offset + tile_size]  7.85 us
    dot_general x2, matrix products, local(): jnp.einsum('hqk,qhd->khd', softmax_low, grad_tile, preferred_element_type...  7.57 us
  transfers between devices with their start and end apart: 12, of which 4 were waited for; matrix products, arithmetic and copies ran while one was open for 37% of the time, Pallas kernels for 0%

profile of v1, /device:TPU:0, one launch (start us, length us, event | category | flops | bytes accessed | tf_op | source)
XLA Modules:
  0.0 218.1 jit_solution(11496503159226749578)
XLA Ops:
  7.2 0.7 all-gather.2.cloned.1.call-update
  7.9 0.5 collective-permute-start.2
  8.5 1.3 copy.38
  9.8 1.3 collective-permute-start.1
  11.1 5.9 %collective-permute-start = (bf16[768,384]{0,1:T(8,128)(2,1)S(1)}, bf16[768,384]{0,1:T(8,128)(2,1)}, u32[]{:S(2)}, u32[]{:S(2)}) collective-permute-start(bf16[768,384]{0,1:T(8,128)(2,1)S(1)} %copy.38), channel_id=1, source_target_pairs={{0,4},{4,8},{8,12},{12,16},{16,20},{20,24},{24,28},{1,5},{5,9},{9,... | collective-permute-start | bytes 1769480 | tf_op jit(solution)/shard_map/ppermute | solution.py:30
  17.0 1.3 copy.44
  18.3 1.3 collective-permute-start.6
  19.6 5.5 %collective-permute-start.5 = (bf16[768,384]{0,1:T(8,128)(2,1)S(1)}, bf16[768,384]{0,1:T(8,128)(2,1)}, u32[]{:S(2)}, u32[]{:S(2)}) collective-permute-start(bf16[768,384]{0,1:T(8,128)(2,1)S(1)} %copy.44), channel_id=1, source_target_pairs={{0,4},{4,8},{8,12},{12,16},{16,20},{20,24},{24,28},{1,5},{5,9},{9,... | collective-permute-start | bytes 1769480 | tf_op jit(solution)/shard_map/ppermute | solution.py:30
  25.0 1.1 fusion.56
  26.2 0.9 copy.94
  27.1 0.9 copy.95
  28.0 2.4 %collective-permute-done.1 = bf16[768,384]{0,1:T(8,128)(2,1)S(1)} collective-permute-done((bf16[768,384]{0,1:T(8,128)(2,1)S(1)}, bf16[768,384]{0,1:T(8,128)(2,1)S(1)}, u32[]{:S(2)}, u32[]{:S(2)}) %collective-permute-start.1) | collective-permute-done | bytes 589856 | tf_op jit(solution)/shard_map/ppermute | solution.py:30
  30.4 1.7 collective-permute-start.4
  32.1 25.0 %collective-permute-done = bf16[768,384]{0,1:T(8,128)(2,1)} collective-permute-done((bf16[768,384]{0,1:T(8,128)(2,1)S(1)}, bf16[768,384]{0,1:T(8,128)(2,1)}, u32[]{:S(2)}, u32[]{:S(2)}) %collective-permute-start) | collective-permute-done | bytes 589856 | tf_op jit(solution)/shard_map/ppermute | solution.py:30
  57.2 1.5 pad_maximum_fusion
  59.0 8.6 %fusion.58 = (f32[3,384]{1,0:T(4,128)S(1)}, f32[3,384,2304]{1,2,0:T(8,128)}) fusion(pred[2304]{0:T(1024)(128)(4,1)S(1)} %pad_add_fusion, bf16[2304,3,128]{0,2,1:T(8,128)(2,1)S(1)} %bitcast.77, bf16[384,3,128]{0,2,1:T(8,128)(2,1)} %bitcast.93), kind=kOutput, calls=%fused_computation.92 | convolution fusion | flops 690096384 | bytes 12688128 | tf_op jit(solution)/shard_map/sub | solution.py:81
  67.7 4.9 %collective-permute-done.5 = bf16[768,384]{0,1:T(8,128)(2,1)} collective-permute-done((bf16[768,384]{0,1:T(8,128)(2,1)S(1)}, bf16[768,384]{0,1:T(8,128)(2,1)}, u32[]{:S(2)}, u32[]{:S(2)}) %collective-permute-start.5) | collective-permute-done | bytes 589856 | tf_op jit(solution)/shard_map/ppermute | solution.py:30
  72.6 2.6 %pad_maximum_fusion.1 = bf16[2304,384]{0,1:T(8,128)(2,1)} fusion(bf16[768,384]{0,1:T(8,128)(2,1)} %collective-permute-done.6, bf16[768,384]{0,1:T(8,128)(2,1)S(1)} %copy.44, bf16[768,384]{0,1:T(8,128)(2,1)} %collective-permute-done.5), kind=kLoop, calls=%fused_computation.37 | loop fusion | flops 5308416 | bytes 3538944 | tf_op jit(solution)/shard_map/concatenate | solution.py:66
  75.1 8.8 %fusion.59 = (f32[3,384]{1,0:T(4,128)S(1)}, f32[3,384,2304]{1,2,0:T(8,128)}) fusion(pred[2304]{0:T(1024)(128)(4,1)} %copy-done.9, bf16[2304,3,128]{0,2,1:T(8,128)(2,1)S(1)} %bitcast.78, bf16[384,3,128]{0,2,1:T(8,128)(2,1)} %bitcast.91), kind=kOutput, calls=%fused_computation.93 | convolution fusion | flops 690096384 | bytes 12688128 | tf_op jit(solution)/shard_map/sub | solution.py:81
  83.9 2.4 %constant_dynamic-update-slice_fusion.7 = bf16[768,6144]{1,0:T(8,128)(2,1)} fusion(bf16[768,768]{1,0:T(8,128)(2,1)} %collective-permute-done.3), kind=kLoop, calls=%fused_computation.83 | loop fusion | bytes 2359296
  86.4 2.5 %constant_dynamic-update-slice_fusion.6 = bf16[768,6144]{1,0:T(8,128)(2,1)} fusion(bf16[768,6144]{1,0:T(8,128)(2,1)} %constant_dynamic-update-slice_fusion.7, bf16[768,768]{1,0:T(8,128)(2,1)} %collective-permute-done.2), kind=kLoop, calls=%fused_computation.82 | loop fusion | bytes 2359296
  88.8 1.2 constant_dynamic-update-slice_fusion.5
  90.0 2.4 %constant_dynamic-update-slice_fusion.4 = bf16[768,6144]{1,0:T(8,128)(2,1)} fusion(bf16[768,6144]{1,0:T(8,128)(2,1)} %constant_dynamic-update-slice_fusion.5, bf16[768,768]{1,0:T(8,128)(2,1)} %collective-permute-done.4), kind=kLoop, calls=%fused_computation.80 | loop fusion | bytes 2359296
  92.4 2.4 %constant_dynamic-update-slice_fusion.3 = bf16[768,6144]{1,0:T(8,128)(2,1)} fusion(bf16[768,6144]{1,0:T(8,128)(2,1)} %constant_dynamic-update-slice_fusion.4, bf16[768,768]{1,0:T(8,128)(2,1)} %collective-permute-done.3), kind=kLoop, calls=%fused_computation.79 | loop fusion | bytes 2359296
  94.8 2.4 %constant_dynamic-update-slice_fusion.2 = bf16[768,6144]{1,0:T(8,128)(2,1)} fusion(bf16[768,6144]{1,0:T(8,128)(2,1)} %constant_dynamic-update-slice_fusion.3, bf16[768,768]{1,0:T(8,128)(2,1)} %collective-permute-done.2), kind=kLoop, calls=%fused_computation.78 | loop fusion | bytes 2359296
  97.2 1.1 constant_dynamic-update-slice_fusion.1
  98.3 2.4 %constant_dynamic-update-slice_fusion = bf16[768,6144]{1,0:T(8,128)(2,1)} fusion(bf16[768,6144]{1,0:T(8,128)(2,1)} %constant_dynamic-update-slice_fusion.1, bf16[768,768]{1,0:T(8,128)(2,1)} %collective-permute-done.4), kind=kLoop, calls=%fused_computation.76 | loop fusion | bytes 2359296 | tf_op jit(solution)/shard_map/jit(_roll_dynamic)/concatenate | solution.py:24
  100.7 5.6 %fusion.30 = bf16[768,384]{0,1:T(8,128)(2,1)S(1)} fusion(bf16[384,3072]{1,0:T(8,128)(2,1)} %all-gather.2.cloned.1.call-done, bf16[768,6144]{1,0:T(8,128)(2,1)} %constant_dynamic-update-slice_fusion, s32[]{:T(128)S(6)} %select_n.36), kind=kOutput, calls=%fused_computation.38 | convolution fusion | flops 1812234240 | bytes 7667716 | tf_op jit(solution)/shard_map/td,hd->th/dot_general | solution.py:46
  106.4 6.0 %fusion.27 = f32[2304,3,128]{0,2,1:T(8,128)S(1)} fusion(bf16[384,3,128]{0,2,1:T(8,128)(2,1)S(1)} %bitcast.107, f32[3,384,2304]{1,2,0:T(8,128)} %get-tuple-element.20, f32[3,384]{1,0:T(4,128)S(1)} %get-tuple-element.19), kind=kOutput, calls=%fused_computation.35 | convolution fusion | flops 684785664 | bytes 14455296 | tf_op jit(solution)/shard_map/hqk,qhd->khd/dot_general | solution.py:101
  112.8 0.6 slice-done.5
  113.9 5.0 %multiply_reduce_fusion = (f32[3,384]{1,0:T(4,128)S(1)}, f32[3,384,2304]{1,2,0:T(8,128)}) fusion(f32[3,384,2304]{1,2,0:T(8,128)S(1)} %bitcast.84, f32[3,384]{1,0:T(4,128)S(1)} %get-tuple-element.19, bf16[384,3,128]{0,2,1:T(8,128)(2,1)S(1)} %bitcast.108, bf16[2304,3,128]{0,2,1:T(8,128)(2,1)S(1)} %bitcast.89), kind=kOutput, calls=%fused_computation.11 | convolution fusion | flops 687438720 | bytes 23307264 | tf_op jit(solution)/shard_map/qhd,khd->hqk/dot_general | solution.py:84
  118.9 8.3 %multiply_convert_fusion = bf16[3,384,2304]{1,2,0:T(8,128)(2,1)S(1)} fusion(f32[3,384,2304]{1,2,0:T(8,128)} %get-tuple-element.22, f32[3,384]{1,0:T(4,128)S(1)} %get-tuple-element.21, f32[3,384,2304]{1,2,0:T(8,128)} %get-tuple-element.20, f32[3,384]{1,0:T(4,128)S(1)} %get-tuple-element.19), kind=kLoop, calls=%fused_computation.10 | loop fusion | flops 10616832 | bytes 26551296 | tf_op jit(solution)/shard_map/convert_element_type | solution.py:88
  127.3 1.9 fusion.34
  129.1 3.4 %fusion.23 = f32[2304,3,128]{0,2,1:T(8,128)} fusion(bf16[3,384,2304]{1,2,0:T(8,128)(2,1)S(1)} %multiply_convert_fusion, bf16[384,3,128]{0,2,1:T(8,128)(2,1)S(1)} %bitcast.94), kind=kOutput, calls=%fused_computation.33 | convolution fusion | flops 680361984 | bytes 9142272 | tf_op jit(solution)/shard_map/hqk,qhd->khd/dot_general | solution.py:97
  132.5 1.6 fusion.24
  134.1 4.9 %multiply_reduce_fusion.1 = (f32[3,384]{1,0:T(4,128)S(1)}, f32[3,384,2304]{1,2,0:T(8,128)}) fusion(f32[3,384,2304]{1,2,0:T(8,128)S(1)} %bitcast.82, f32[3,384]{1,0:T(4,128)S(1)} %get-tuple-element.23, bf16[384,3,128]{0,2,1:T(8,128)(2,1)S(1)} %bitcast.106, bf16[2304,3,128]{0,2,1:T(8,128)(2,1)S(1)} %bitcast.90), kind=kOutput, calls=%fused_computation.14 | convolution fusion | flops 687438720 | bytes 23307264 | tf_op jit(solution)/shard_map/qhd,khd->hqk/dot_general | solution.py:84
  139.0 1.2 fusion.46
  140.2 1.8 copy.74
  142.0 1.8 copy.77
  143.9 0.9 copy.76
  145.0 1.8 pad_maximum_fusion.5
  146.8 1.3 collective-permute-start.9
  148.1 1.9 pad_maximum_fusion.6
  150.1 6.0 %collective-permute-start.10 = (bf16[768,384]{1,0:T(8,128)(2,1)}, bf16[768,384]{1,0:T(8,128)(2,1)}, u32[]{:S(2)}, u32[]{:S(2)}) collective-permute-start(bf16[768,384]{1,0:T(8,128)(2,1)} %pad_maximum_fusion.6), channel_id=1, source_target_pairs={{0,4},{4,8},{8,12},{12,16},{16,20},{20,24},{24,28},{1,5},{5,9},{9,... | collective-permute-start | bytes 1769480 | tf_op jit(solution)/shard_map/ppermute | solution.py:30
  156.1 8.0 %multiply_convert_fusion.1 = bf16[3,384,2304]{1,2,0:T(8,128)(2,1)S(1)} fusion(f32[3,384,2304]{1,2,0:T(8,128)} %get-tuple-element.26, f32[3,384]{1,0:T(4,128)S(1)} %get-tuple-element.25, f32[3,384,2304]{1,2,0:T(8,128)} %get-tuple-element.24, f32[3,384]{1,0:T(4,128)S(1)} %get-tuple-element.23), kind=kLoop, calls=%fused_computation.13 | loop fusion | flops 10616832 | bytes 26551296 | tf_op jit(solution)/shard_map/convert_element_type | solution.py:88
  164.1 1.6 fusion.22
  165.7 1.1 copy-done
  166.8 1.2 copy-done.1
  168.0 1.4 fusion.50
  169.4 1.8 copy.66
  171.2 1.9 copy.69
  173.1 1.8 copy.68
  174.9 1.8 copy.67
  176.8 1.9 pad_maximum_fusion.3
  178.7 1.3 collective-permute-start.7
  180.0 1.9 pad_maximum_fusion.4
  181.9 5.7 %collective-permute-start.8 = (bf16[768,384]{1,0:T(8,128)(2,1)}, bf16[768,384]{1,0:T(8,128)(2,1)}, u32[]{:S(2)}, u32[]{:S(2)}) collective-permute-start(bf16[768,384]{1,0:T(8,128)(2,1)} %pad_maximum_fusion.4), channel_id=1, source_target_pairs={{0,4},{4,8},{8,12},{12,16},{16,20},{20,24},{24,28},{1,5},{5,9},{9,... | collective-permute-start | bytes 1769480 | tf_op jit(solution)/shard_map/ppermute | solution.py:30
  187.6 4.3 %fusion.33 = bf16[3,128,384]{2,1,0:T(8,128)(2,1)} fusion(bf16[2304,3,128]{0,2,1:T(8,128)(2,1)S(1)} %bitcast.80, bf16[3,384,2304]{1,2,0:T(8,128)(2,1)} %copy-done), kind=kOutput, calls=%fused_computation.41 | convolution fusion | flops 679772160 | bytes 7372800 | tf_op jit(solution)/shard_map/hqk,khd->qhd/dot_general | solution.py:91
  191.9 1.9 copy.61
  194.3 1.2 copy.60
  196.0 1.8 pad_maximum_fusion.2
  197.8 2.2 %fusion.38 = bf16[768,384]{1,0:T(8,128)(2,1)} fusion(f32[384,384]{1,0:T(8,128)S(1)} %copy.73, f32[384,384]{1,0:T(8,128)S(1)} %copy.72, bf16[768,384]{1,0:T(8,128)(2,1)} %collective-permute-done.10, bf16[768,384]{1,0:T(8,128)(2,1)} %collective-permute-done.9), kind=kLoop, calls=%fused_computation.48 | loop fusion | flops 1769472 | bytes 2949120 | tf_op jit(solution)/shard_map/convert_element_type | solution.py:135
  200.1 8.9 %collective-permute-done.8 = bf16[768,384]{1,0:T(8,128)(2,1)} collective-permute-done((bf16[768,384]{1,0:T(8,128)(2,1)}, bf16[768,384]{1,0:T(8,128)(2,1)}, u32[]{:S(2)}, u32[]{:S(2)}) %collective-permute-start.8) | collective-permute-done | bytes 589856 | tf_op jit(solution)/shard_map/ppermute | solution.py:30
  209.0 2.2 %fusion.36 = bf16[768,384]{1,0:T(8,128)(2,1)} fusion(f32[384,384]{1,0:T(8,128)S(1)} %copy.65, f32[384,384]{1,0:T(8,128)S(1)} %copy.64, bf16[768,384]{1,0:T(8,128)(2,1)} %collective-permute-done.8, bf16[768,384]{1,0:T(8,128)(2,1)} %collective-permute-done.7), kind=kLoop, calls=%fused_computation.45 | loop fusion | flops 1769472 | bytes 2949120 | tf_op jit(solution)/shard_map/convert_element_type | solution.py:135
  (51 shorter events, 2.6 us)
Async XLA Ops:
  7.2 23.2 %copy-start.2 = (bf16[768,768]{1,0:T(8,128)(2,1)S(1)}, bf16[768,768]{1,0:T(8,128)(2,1)}, u32[]{:S(2)}) copy-start(bf16[768,768]{1,0:T(8,128)(2,1)} %param.8) | copy-start | bytes 3538948
  7.2 93.6 %all-gather.2.cloned.1.call-start = ((), (), s32[]{:S(2)}) async-start(), calls=%async_computation | async-start | bytes 2654208 | tf_op jit(solution)/shard_map/all_gather | solution.py:49
  7.9 50.8 %collective-permute-start.2 = (bf16[768,768]{1,0:T(8,128)(2,1)}, bf16[768,768]{1,0:T(8,128)(2,1)}, u32[]{:S(2)}, u32[]{:S(2)}) collective-permute-start(bf16[768,768]{1,0:T(8,128)(2,1)} %param.8), channel_id=1, source_target_pairs={{0,1},{1,2},{2,3},{3,0},{4,5},{5,6},{6,7},{7,4},{8,9},{9,10},{10,1... | collective-permute-start | bytes 3538952 | tf_op jit(solution)/shard_map/ppermute | solution.py:20
  9.8 22.4 %copy-start.4 = (bf16[768,384]{0,1:T(8,128)(2,1)}, bf16[768,384]{0,1:T(8,128)(2,1)S(1)}, u32[]{:S(2)}) copy-start(bf16[768,384]{0,1:T(8,128)(2,1)S(1)} %copy.38) | copy-start | bytes 1769476
  9.8 20.6 %collective-permute-start.1 = (bf16[768,384]{0,1:T(8,128)(2,1)S(1)}, bf16[768,384]{0,1:T(8,128)(2,1)S(1)}, u32[]{:S(2)}, u32[]{:S(2)}) collective-permute-start(bf16[768,384]{0,1:T(8,128)(2,1)S(1)} %copy.38), channel_id=1, source_target_pairs={{4,0},{8,4},{12,8},{16,12},{20,16},{24,20},{28,24},{5,1},{9,5},{13... | collective-permute-start | bytes 1769480 | tf_op jit(solution)/shard_map/ppermute | solution.py:30
  11.1 46.1 %collective-permute-start = (bf16[768,384]{0,1:T(8,128)(2,1)S(1)}, bf16[768,384]{0,1:T(8,128)(2,1)}, u32[]{:S(2)}, u32[]{:S(2)}) collective-permute-start(bf16[768,384]{0,1:T(8,128)(2,1)S(1)} %copy.38), channel_id=1, source_target_pairs={{0,4},{4,8},{8,12},{12,16},{16,20},{20,24},{24,28},{1,5},{5,9},{9,... | collective-permute-start | bytes 1769480 | tf_op jit(solution)/shard_map/ppermute | solution.py:30
  18.3 49.4 %collective-permute-start.6 = (bf16[768,384]{0,1:T(8,128)(2,1)S(1)}, bf16[768,384]{0,1:T(8,128)(2,1)}, u32[]{:S(2)}, u32[]{:S(2)}) collective-permute-start(bf16[768,384]{0,1:T(8,128)(2,1)S(1)} %copy.44), channel_id=1, source_target_pairs={{4,0},{8,4},{12,8},{16,12},{20,16},{24,20},{28,24},{5,1},{9,5},{13... | collective-permute-start | bytes 1769480 | tf_op jit(solution)/shard_map/ppermute | solution.py:30
  19.6 53.0 %collective-permute-start.5 = (bf16[768,384]{0,1:T(8,128)(2,1)S(1)}, bf16[768,384]{0,1:T(8,128)(2,1)}, u32[]{:S(2)}, u32[]{:S(2)}) collective-permute-start(bf16[768,384]{0,1:T(8,128)(2,1)S(1)} %copy.44), channel_id=1, source_target_pairs={{0,4},{4,8},{8,12},{12,16},{16,20},{20,24},{24,28},{1,5},{5,9},{9,... | collective-permute-start | bytes 1769480 | tf_op jit(solution)/shard_map/ppermute | solution.py:30
  28.0 39.7 %copy-start.9 = (pred[2304]{0:T(1024)(128)(4,1)}, pred[2304]{0:T(1024)(128)(4,1)S(1)}, u32[]{:S(2)}) copy-start(pred[2304]{0:T(1024)(128)(4,1)S(1)} %pad_add_fusion) | copy-start | bytes 6916
  30.4 1.7 copy-start.8
  30.4 59.6 %collective-permute-start.4 = (bf16[768,768]{1,0:T(8,128)(2,1)S(1)}, bf16[768,768]{1,0:T(8,128)(2,1)}, u32[]{:S(2)}, u32[]{:S(2)}) collective-permute-start(bf16[768,768]{1,0:T(8,128)(2,1)S(1)} %copy-done.2), channel_id=1, source_target_pairs={{0,3},{1,0},{2,1},{3,2},{4,7},{5,4},{6,5},{7,6},{8,11},{9,8},{10,9... | collective-permute-start | bytes 3538952 | tf_op jit(solution)/shard_map/ppermute | solution.py:22
  58.7 25.2 %collective-permute-start.3 = (bf16[768,768]{1,0:T(8,128)(2,1)}, bf16[768,768]{1,0:T(8,128)(2,1)}, u32[]{:S(2)}, u32[]{:S(2)}) collective-permute-start(bf16[768,768]{1,0:T(8,128)(2,1)} %collective-permute-done.2), channel_id=1, source_target_pairs={{0,1},{1,2},{2,3},{3,0},{4,5},{5,6},{6,7},{7,4},{8,9},{9,10},{10,1... | collective-permute-start | bytes 3538952 | tf_op jit(solution)/shard_map/ppermute | solution.py:20
  106.3 6.1 %slice-start.3 = ((s8[10616832]{0:T(1024)(128)(4,1)}), s8[4194304]{0:T(1024)(128)(4,1)S(1)}, s32[]{:S(2)}) async-start(s8[10616832]{0:T(1024)(128)(4,1)} %bitcast.83), calls=%async_computation.4 | async-start | bytes 8388608
  106.4 6.4 %slice-start.4 = ((s8[10616832]{0:T(1024)(128)(4,1)}), s8[4194304]{0:T(1024)(128)(4,1)S(1)}, s32[]{:S(2)}) async-start(s8[10616832]{0:T(1024)(128)(4,1)} %bitcast.83), calls=%async_computation.5 | async-start | bytes 8388608
  106.4 7.1 %slice-start.5 = ((s8[10616832]{0:T(1024)(128)(4,1)}), s8[2228224]{0:T(1024)(128)(4,1)S(1)}, s32[]{:S(2)}) async-start(s8[10616832]{0:T(1024)(128)(4,1)} %bitcast.83), calls=%async_computation.6 | async-start | bytes 4456448
  106.4 7.5 %copy-start.5 = (bf16[2304,384]{0,1:T(8,128)(2,1)S(1)}, bf16[2304,384]{0,1:T(8,128)(2,1)}, u32[]{:S(2)}) copy-start(bf16[2304,384]{0,1:T(8,128)(2,1)} %pad_maximum_fusion.1) | copy-start | bytes 5308420
  118.9 13.6 %slice-start = ((s8[10616832]{0:T(1024)(128)(4,1)}), s8[4194304]{0:T(1024)(128)(4,1)S(1)}, s32[]{:S(2)}) async-start(s8[10616832]{0:T(1024)(128)(4,1)} %bitcast.81), calls=%async_computation.1 | async-start | bytes 8388608
  118.9 13.6 %slice-start.1 = ((s8[10616832]{0:T(1024)(128)(4,1)}), s8[4194304]{0:T(1024)(128)(4,1)S(1)}, s32[]{:S(2)}) async-start(s8[10616832]{0:T(1024)(128)(4,1)} %bitcast.81), calls=%async_computation.2 | async-start | bytes 8388608
  127.2 1.9 copy-start.7
  127.2 5.2 %slice-start.2 = ((s8[10616832]{0:T(1024)(128)(4,1)}), s8[2228224]{0:T(1024)(128)(4,1)S(1)}, s32[]{:S(2)}) async-start(s8[10616832]{0:T(1024)(128)(4,1)} %bitcast.81), calls=%async_computation.3 | async-start | bytes 4456448
  146.8 51.0 %collective-permute-start.9 = (bf16[768,384]{1,0:T(8,128)(2,1)}, bf16[768,384]{1,0:T(8,128)(2,1)}, u32[]{:S(2)}, u32[]{:S(2)}) collective-permute-start(bf16[768,384]{1,0:T(8,128)(2,1)} %pad_maximum_fusion.5), channel_id=1, source_target_pairs={{4,0},{8,4},{12,8},{16,12},{20,16},{24,20},{28,24},{5,1},{9,5},{13... | collective-permute-start | bytes 1769480 | tf_op jit(solution)/shard_map/ppermute | solution.py:30
  150.1 47.7 %collective-permute-start.10 = (bf16[768,384]{1,0:T(8,128)(2,1)}, bf16[768,384]{1,0:T(8,128)(2,1)}, u32[]{:S(2)}, u32[]{:S(2)}) collective-permute-start(bf16[768,384]{1,0:T(8,128)(2,1)} %pad_maximum_fusion.6), channel_id=1, source_target_pairs={{0,4},{4,8},{8,12},{12,16},{16,20},{20,24},{24,28},{1,5},{5,9},{9,... | collective-permute-start | bytes 1769480 | tf_op jit(solution)/shard_map/ppermute | solution.py:30
  156.1 8.0 %copy-start.6 = (bf16[384,384]{0,1:T(8,128)(2,1)S(1)}, bf16[384,384]{0,1:T(8,128)(2,1)}, u32[]{:S(2)}) copy-start(bf16[384,384]{0,1:T(8,128)(2,1)} %copy.94) | copy-start | bytes 884740
  164.1 2.7 %copy-start = (bf16[3,384,2304]{1,2,0:T(8,128)(2,1)}, bf16[3,384,2304]{1,2,0:T(8,128)(2,1)S(1)}, u32[]{:S(2)}) copy-start(bf16[3,384,2304]{1,2,0:T(8,128)(2,1)S(1)} %multiply_convert_fusion.1) | copy-start | bytes 15925252
  164.1 3.9 %copy-start.1 = (f32[2304,3,128]{0,2,1:T(8,128)S(1)}, f32[2304,3,128]{0,2,1:T(8,128)}, u32[]{:S(2)}) copy-start(f32[2304,3,128]{0,2,1:T(8,128)} %fusion.23) | copy-start | bytes 10616836
  178.7 21.4 %collective-permute-start.7 = (bf16[768,384]{1,0:T(8,128)(2,1)}, bf16[768,384]{1,0:T(8,128)(2,1)}, u32[]{:S(2)}, u32[]{:S(2)}) collective-permute-start(bf16[768,384]{1,0:T(8,128)(2,1)} %pad_maximum_fusion.3), channel_id=1, source_target_pairs={{4,0},{8,4},{12,8},{16,12},{20,16},{24,20},{28,24},{5,1},{9,5},{13... | collective-permute-start | bytes 1769480 | tf_op jit(solution)/shard_map/ppermute | solution.py:30
  181.9 27.1 %collective-permute-start.8 = (bf16[768,384]{1,0:T(8,128)(2,1)}, bf16[768,384]{1,0:T(8,128)(2,1)}, u32[]{:S(2)}, u32[]{:S(2)}) collective-permute-start(bf16[768,384]{1,0:T(8,128)(2,1)} %pad_maximum_fusion.4), channel_id=1, source_target_pairs={{0,4},{4,8},{8,12},{12,16},{16,20},{20,24},{24,28},{1,5},{5,9},{9,... | collective-permute-start | bytes 1769480 | tf_op jit(solution)/shard_map/ppermute | solution.py:30
  191.9 3.6 %copy-start.3 = (f32[384,3,128]{0,2,1:T(8,128)S(1)}, f32[384,3,128]{0,2,1:T(8,128)}, u32[]{:S(2)}) copy-start(f32[384,3,128]{0,2,1:T(8,128)} %get-tuple-element.13) | copy-start | bytes 1769476
Sparse Core Ops, SparseCore 0:
  10.0 82.9 all-gather.1
